TPU v7x, 32 devices: a whole 2x2x4 slice. The times are simulated.
32 devices in a mesh: dp: 8 (over z, core), tensor: 4 (over y, x).
Axes of the slice: x: 2, y: 2, z: 4, core: 2. Of those that a mesh axis runs over, the one named last changes fastest.
Arguments:
- tokens: bfloat16 [16384, 2048], P(('dp', 'tensor')), may hold values from -6 to 6
- cotangent: bfloat16 [16384, 2048], P(('dp', 'tensor')), may hold values from -12 to 12
- lengths: int32 [8], P('dp'), may hold values from 512 to 2048, as said below
- query_weight: bfloat16 [2048, 2048], P('dp', 'tensor'), may hold values from -0.125 to 0.125
- key_weight: bfloat16 [2048, 2048], P('dp', 'tensor'), may hold values from -0.125 to 0.125
- value_weight: bfloat16 [2048, 2048], P('dp', 'tensor'), may hold values from -0.125 to 0.125
- out_weight: bfloat16 [2048, 2048], P('dp', 'tensor'), may hold values from -3 to 3
- up_weight: bfloat16 [2048, 8192], P('dp', 'tensor'), may hold values from -0.125 to 0.125
- down_weight: bfloat16 [2048, 8192], P('dp', 'tensor'), may hold values from -0.0625 to 0.0625
- query_bias: float32 [2048], replicated, may hold values from -1.25 to 1.25
- value_bias: float32 [2048], replicated, may hold values from -0.0625 to 0.0625
- out_bias: float32 [2048], replicated, may hold values from -0.625 to 0.625
- norm1_gain: float32 [2048], replicated, may hold values from 0.5 to 1.5
- norm1_shift: float32 [2048], replicated, may hold values from -0.625 to 0.625
- up_bias: float32 [8192], replicated, may hold values from -0.625 to 0.625
- down_bias: float32 [2048], replicated, may hold values from -0.625 to 0.625
- norm2_gain: float32 [2048], replicated, may hold values from 0.5 to 1.5
- norm2_shift: float32 [2048], replicated, may hold values from -0.625 to 0.625
Outputs:
- layer_out: bfloat16 [16384, 2048], P(('dp', 'tensor'))
- tokens_grad: bfloat16 [16384, 2048], P(('dp', 'tensor'))
- query_weight_grad: float32 [2048, 2048], P('dp', 'tensor')
- key_weight_grad: float32 [2048, 2048], P('dp', 'tensor')
- value_weight_grad: float32 [2048, 2048], P('dp', 'tensor')
- out_weight_grad: float32 [2048, 2048], P('dp', 'tensor')
- up_weight_grad: float32 [2048, 8192], P('dp', 'tensor')
- down_weight_grad: float32 [2048, 8192], P('dp', 'tensor')
- query_bias_grad: float32 [2048], P(('dp', 'tensor'))
- value_bias_grad: float32 [2048], P(('dp', 'tensor'))
- out_bias_grad: float32 [2048], P(('dp', 'tensor'))
- norm1_gain_grad: float32 [2048], P(('dp', 'tensor'))
- norm1_shift_grad: float32 [2048], P(('dp', 'tensor'))
- up_bias_grad: float32 [8192], P(('dp', 'tensor'))
- down_bias_grad: float32 [2048], P(('dp', 'tensor'))
- norm2_gain_grad: float32 [2048], P(('dp', 'tensor'))
- norm2_shift_grad: float32 [2048], P(('dp', 'tensor'))
Inputs may be any that keep to these rules, and one draw needn't show every extreme that they name: `lengths`: in every draw one slot holds a sequence of the full 2048 tokens.
All inputs are finite; a program needn't handle non-finite values.
Results may differ from a plain program's by a relative error of at most 0.025.
Values may be sent and summed in bfloat16 or wider, within the bound.
No kernel may reach another device: no remote copies, remote signals or barrier semaphores. Data moves between devices by JAX's collectives and lax.ppermute only.
A program may use at most 256 MiB of HBM per device.

v0:
```python
import jax
import jax.numpy as jnp
from jax import lax
from jax.sharding import PartitionSpec as P

HEADS = 16
HEAD_DIM = 128
FF = 8192
norm_eps = 1e-06
masked_score = -1e30


def contract_rows(left, right):
    return lax.dot_general(
        left, right, (((0,), (0,)), ((), ())), preferred_element_type=jnp.float32
    )


def contract_cols(left, right):
    return lax.dot_general(
        left, right, (((1,), (1,)), ((), ())), preferred_element_type=jnp.float32
    )


def norm_rows(value, gain, shift):
    centred = value - jnp.mean(value, axis=-1, keepdims=True)
    inverse = lax.rsqrt(jnp.mean(centred * centred, axis=-1, keepdims=True) + norm_eps)
    unit = centred * inverse
    return (unit * gain + shift, unit, inverse)


def norm_back(grad_out, unit, inverse, gain):
    grad_unit = grad_out * gain
    inner = jnp.mean(grad_unit * unit, axis=-1, keepdims=True)
    grad_in = inverse * (grad_unit - jnp.mean(grad_unit, axis=-1, keepdims=True) - unit * inner)
    return (grad_in, jnp.sum(grad_out * unit, axis=0), jnp.sum(grad_out, axis=0))


def smooth_gate(value):
    return jax.nn.gelu(value, approximate=True)


def placed(part, start, total):
    return lax.dynamic_update_slice_in_dim(jnp.zeros((total,), jnp.float32), part, start, 0)


def per_device(
    tokens,
    cotangent,
    lengths,
    query_weight,
    key_weight,
    value_weight,
    out_weight,
    up_weight,
    down_weight,
    query_bias,
    value_bias,
    out_bias,
    norm1_gain,
    norm1_shift,
    up_bias,
    down_bias,
    norm2_gain,
    norm2_shift,
):
    rows = tokens.shape[0]
    width = tokens.shape[1]
    groups = lax.axis_size("tensor")
    position = lax.axis_index("tensor")
    seq_len = rows * groups
    head_count = HEADS // groups
    head_cols = width // groups
    hidden_cols = FF // groups
    scale = HEAD_DIM ** (-0.5)
    slot_len = lengths[0]
    key_live = jnp.arange(seq_len, dtype=jnp.int32) < slot_len
    row_live = (position * rows + jnp.arange(rows, dtype=jnp.int32) < slot_len).astype(jnp.float32)[
        :, None
    ]
    col_start = position * head_cols
    hid_start = position * hidden_cols
    bias_query = lax.dynamic_slice_in_dim(query_bias, col_start, head_cols)
    bias_value = lax.dynamic_slice_in_dim(value_bias, col_start, head_cols)
    bias_up = lax.dynamic_slice_in_dim(up_bias, hid_start, hidden_cols)
    query_full, key_full, value_full, out_full = (
        lax.all_gather(query_weight, "dp", axis=0, tiled=True),
        lax.all_gather(key_weight, "dp", axis=0, tiled=True),
        lax.all_gather(value_weight, "dp", axis=0, tiled=True),
        lax.all_gather(out_weight, "dp", axis=0, tiled=True),
    )
    piece = lax.all_gather(tokens, "tensor", axis=0, tiled=True)
    queries = (jnp.dot(piece, query_full, preferred_element_type=jnp.float32) + bias_query).astype(
        jnp.bfloat16
    )
    keys = jnp.dot(piece, key_full, preferred_element_type=jnp.float32).astype(jnp.bfloat16)
    values = (jnp.dot(piece, value_full, preferred_element_type=jnp.float32) + bias_value).astype(
        jnp.bfloat16
    )
    seq_tokens, queries, keys, values = (piece, queries, keys, values)
    block = min(512, seq_len)
    blocks = seq_len // block
    key_heads = keys.reshape(seq_len, head_count, HEAD_DIM)
    value_heads = values.reshape(seq_len, head_count, HEAD_DIM)
    query_blocks = queries.reshape(blocks, block, head_count, HEAD_DIM)

    def scores_of(query_block):
        raw = (
            jnp.einsum("qhd,khd->hqk", query_block, key_heads, preferred_element_type=jnp.float32)
            * scale
        )
        return jnp.where(key_live, raw, masked_score)

    def attend(query_block):
        scores = scores_of(query_block)
        highest = jnp.max(scores, axis=-1, keepdims=True)
        normal = highest + jnp.log(jnp.sum(jnp.exp(scores - highest), axis=-1, keepdims=True))
        probs = jnp.exp(scores - normal).astype(jnp.bfloat16)
        context = jnp.einsum("hqk,khd->qhd", probs, value_heads, preferred_element_type=jnp.float32)
        return (context.astype(jnp.bfloat16), normal)

    context_blocks, totals = lax.map(attend, query_blocks)
    context = context_blocks.reshape(seq_len, head_cols)
    attn_sum = lax.psum_scatter(
        contract_cols(context, out_full).astype(jnp.bfloat16),
        "tensor",
        scatter_dimension=0,
        tiled=True,
    ).astype(jnp.float32)
    mid, mid_unit, mid_inverse = norm_rows(
        tokens.astype(jnp.float32) + attn_sum + out_bias, norm1_gain, norm1_shift
    )
    mid_low = mid.astype(jnp.bfloat16)
    up_full, down_full = (
        lax.all_gather(up_weight, "dp", axis=0, tiled=True),
        lax.all_gather(down_weight, "dp", axis=0, tiled=True),
    )
    piece = lax.all_gather(mid_low, "tensor", axis=0, tiled=True)
    pre = jnp.dot(piece, up_full, preferred_element_type=jnp.float32) + bias_up
    mid_seq = piece
    activ = smooth_gate(pre).astype(jnp.bfloat16)
    ffn_sum = lax.psum_scatter(
        contract_cols(activ, down_full).astype(jnp.bfloat16),
        "tensor",
        scatter_dimension=0,
        tiled=True,
    ).astype(jnp.float32)
    final, final_unit, final_inverse = norm_rows(mid + ffn_sum + down_bias, norm2_gain, norm2_shift)
    layer_out = (final * row_live).astype(jnp.bfloat16)
    grad_final = cotangent.astype(jnp.float32) * row_live
    grad_sum2, norm2_gain_grad, norm2_shift_grad = norm_back(
        grad_final, final_unit, final_inverse, norm2_gain
    )
    down_bias_grad = jnp.sum(grad_sum2, axis=0)
    piece = lax.all_gather(grad_sum2.astype(jnp.bfloat16), "tensor", axis=0, tiled=True)
    grad_act = jnp.dot(piece, down_full, preferred_element_type=jnp.float32)
    unused, gate_back = jax.vjp(smooth_gate, pre)
    grad_ffn = piece
    grad_pre = gate_back(grad_act)[0].astype(jnp.bfloat16)
    down_grad = contract_rows(grad_ffn, activ)
    up_grad = contract_rows(mid_seq, grad_pre)
    up_bias_part = jnp.sum(grad_pre.astype(jnp.float32), axis=0)
    grad_mid = grad_sum2 + lax.psum_scatter(
        contract_cols(grad_pre, up_full).astype(jnp.bfloat16),
        "tensor",
        scatter_dimension=0,
        tiled=True,
    ).astype(jnp.float32)
    grad_sum1, norm1_gain_grad, norm1_shift_grad = norm_back(
        grad_mid, mid_unit, mid_inverse, norm1_gain
    )
    out_bias_grad = jnp.sum(grad_sum1, axis=0)
    piece = lax.all_gather(grad_sum1.astype(jnp.bfloat16), "tensor", axis=0, tiled=True)
    grad_context = jnp.dot(piece, out_full, preferred_element_type=jnp.float32).astype(jnp.bfloat16)
    out_grad = contract_rows(piece, context)
    grad_context_blocks = grad_context.reshape(blocks, block, head_count, HEAD_DIM)

    def attend_back(carry, item):
        key_acc, value_acc = carry
        query_block, grad_block, normal = item
        probs = jnp.exp(scores_of(query_block) - normal)
        grad_probs = jnp.einsum(
            "qhd,khd->hqk", grad_block, value_heads, preferred_element_type=jnp.float32
        )
        inner = jnp.sum(probs * grad_probs, axis=-1, keepdims=True)
        grad_scores = (probs * (grad_probs - inner)).astype(jnp.bfloat16)
        grad_query = (
            jnp.einsum("hqk,khd->qhd", grad_scores, key_heads, preferred_element_type=jnp.float32)
            * scale
        )
        key_acc = (
            key_acc
            + jnp.einsum(
                "hqk,qhd->khd", grad_scores, query_block, preferred_element_type=jnp.float32
            )
            * scale
        )
        value_acc = value_acc + jnp.einsum(
            "hqk,qhd->khd",
            probs.astype(jnp.bfloat16),
            grad_block,
            preferred_element_type=jnp.float32,
        )
        return ((key_acc, value_acc), grad_query.astype(jnp.bfloat16))

    zero_heads = jnp.zeros((seq_len, head_count, HEAD_DIM), jnp.float32)
    (key_acc, value_acc), grad_query_blocks = lax.scan(
        attend_back, (zero_heads, zero_heads), (query_blocks, grad_context_blocks, totals)
    )
    grad_queries = grad_query_blocks.reshape(seq_len, head_cols)
    grad_keys = key_acc.reshape(seq_len, head_cols).astype(jnp.bfloat16)
    grad_values = value_acc.reshape(seq_len, head_cols).astype(jnp.bfloat16)
    query_grad = contract_rows(seq_tokens, grad_queries)
    key_grad = contract_rows(seq_tokens, grad_keys)
    value_grad = contract_rows(seq_tokens, grad_values)
    query_bias_part = jnp.sum(grad_queries.astype(jnp.float32), axis=0)
    value_bias_part = jnp.sum(grad_values.astype(jnp.float32), axis=0)
    total = contract_cols(grad_queries, query_full)
    total = total + contract_cols(grad_keys, key_full)
    tokens_grad = (
        grad_sum1
        + lax.psum_scatter(
            (total + contract_cols(grad_values, value_full)).astype(jnp.bfloat16),
            "tensor",
            scatter_dimension=0,
            tiled=True,
        ).astype(jnp.float32)
    ).astype(jnp.bfloat16)
    query_part, key_part, value_part, out_part, up_part, down_part = (
        lax.psum_scatter(
            query_grad.astype(jnp.bfloat16), "dp", scatter_dimension=0, tiled=True
        ).astype(jnp.float32),
        lax.psum_scatter(
            key_grad.astype(jnp.bfloat16), "dp", scatter_dimension=0, tiled=True
        ).astype(jnp.float32),
        lax.psum_scatter(
            value_grad.astype(jnp.bfloat16), "dp", scatter_dimension=0, tiled=True
        ).astype(jnp.float32),
        lax.psum_scatter(
            out_grad.astype(jnp.bfloat16), "dp", scatter_dimension=0, tiled=True
        ).astype(jnp.float32),
        lax.psum_scatter(
            up_grad.astype(jnp.bfloat16), "dp", scatter_dimension=0, tiled=True
        ).astype(jnp.float32),
        lax.psum_scatter(
            down_grad.astype(jnp.bfloat16), "dp", scatter_dimension=0, tiled=True
        ).astype(jnp.float32),
    )
    (
        query_bias_grad,
        value_bias_grad,
        out_bias_sum,
        norm1_gain_sum,
        norm1_shift_sum,
        up_bias_grad,
        down_bias_sum,
        norm2_gain_sum,
        norm2_shift_sum,
    ) = (
        lax.psum_scatter(
            placed(query_bias_part, col_start, width),
            ("dp", "tensor"),
            scatter_dimension=0,
            tiled=True,
        ),
        lax.psum_scatter(
            placed(value_bias_part, col_start, width),
            ("dp", "tensor"),
            scatter_dimension=0,
            tiled=True,
        ),
        lax.psum_scatter(out_bias_grad, ("dp", "tensor"), scatter_dimension=0, tiled=True),
        lax.psum_scatter(norm1_gain_grad, ("dp", "tensor"), scatter_dimension=0, tiled=True),
        lax.psum_scatter(norm1_shift_grad, ("dp", "tensor"), scatter_dimension=0, tiled=True),
        lax.psum_scatter(
            placed(up_bias_part, hid_start, FF), ("dp", "tensor"), scatter_dimension=0, tiled=True
        ),
        lax.psum_scatter(down_bias_grad, ("dp", "tensor"), scatter_dimension=0, tiled=True),
        lax.psum_scatter(norm2_gain_grad, ("dp", "tensor"), scatter_dimension=0, tiled=True),
        lax.psum_scatter(norm2_shift_grad, ("dp", "tensor"), scatter_dimension=0, tiled=True),
    )
    return (
        layer_out,
        tokens_grad,
        query_part,
        key_part,
        value_part,
        out_part,
        up_part,
        down_part,
        query_bias_grad,
        value_bias_grad,
        out_bias_sum,
        norm1_gain_sum,
        norm1_shift_sum,
        up_bias_grad,
        down_bias_sum,
        norm2_gain_sum,
        norm2_shift_sum,
    )


def solution(mesh):
    placed = (
        P(("dp", "tensor"), None),
        P(("dp", "tensor"), None),
        P("dp"),
        P("dp", "tensor"),
        P("dp", "tensor"),
        P("dp", "tensor"),
        P("dp", "tensor"),
        P("dp", "tensor"),
        P("dp", "tensor"),
        P(),
        P(),
        P(),
        P(),
        P(),
        P(),
        P(),
        P(),
        P(),
    )
    return jax.shard_map(
        per_device,
        mesh=mesh,
        in_specs=placed,
        out_specs=(
            P(("dp", "tensor"), None),
            P(("dp", "tensor"), None),
            P("dp", "tensor"),
            P("dp", "tensor"),
            P("dp", "tensor"),
            P("dp", "tensor"),
            P("dp", "tensor"),
            P("dp", "tensor"),
            P(("dp", "tensor")),
            P(("dp", "tensor")),
            P(("dp", "tensor")),
            P(("dp", "tensor")),
            P(("dp", "tensor")),
            P(("dp", "tensor")),
            P(("dp", "tensor")),
            P(("dp", "tensor")),
            P(("dp", "tensor")),
        ),
        check_vma=False,
    )
```

profile of v0, /device:TPU:0, one launch (start us, length us, event | category | flops | bytes accessed | tf_op | source)
XLA Modules:
  0.0 1707.2 jit_solution(15198329520281651258)
XLA Ops:
  12.2 29.3 %all-gather.17.cloned.1.call-done = bf16[2048,512]{1,0:T(8,128)(2,1)} async-done(((bf16[256,512]{1,0:T(8,128)(2,1)}), bf16[2048,512]{1,0:T(8,128)(2,1)}) %all-gather.17.cloned.1.call-update) | async-done | bytes 2097168 | tf_op jit(solution)/shard_map/all_gather | solution.py:89
  41.5 88.7 %all-gather.11.cloned.1.call-done = bf16[2048,2048]{1,0:T(8,128)(2,1)} async-done(((bf16[512,2048]{1,0:T(8,128)(2,1)}), bf16[2048,2048]{1,0:T(8,128)(2,1)}) %all-gather.11.cloned.1.call-update) | async-done | bytes 8388624 | tf_op jit(solution)/shard_map/all_gather | solution.py:92
  141.5 19.5 %all-gather.13.cloned.1.call-done = bf16[2048,512]{1,0:T(8,128)(2,1)} async-done(((bf16[256,512]{1,0:T(8,128)(2,1)}), bf16[2048,512]{1,0:T(8,128)(2,1)}) %all-gather.13.cloned.1.call-update) | async-done | bytes 2097168 | tf_op jit(solution)/shard_map/all_gather | solution.py:87
  161.0 9.8 add_convert_fusion.3
  175.1 16.0 all-gather.15.cloned.1.call-done
  191.1 9.9 convolution_convert_fusion.10
  204.0 87.2 %while.28 = (s32[]{:T(128)}, bf16[4,512,4,128]{3,2,1,0:T(4,128)(2,1)}, f32[4,4,512,1]{2,1,3,0:T(4,128)}, bf16[4,512,4,128]{3,1,2,0:T(8,128)(2,1)}, bf16[2048,4,1...) while((s32[]{:T(128)}, bf16[4,512,4,128]{3,2,1,0:T(4,128)(2,1)}, ...), condition=%wide.region_3.4_spmd.clone, body=%wide.region_0.3_spmd.clone.sunk | while | flops 2193883136 | bytes 132194472 | solution.py:122
  215.8 9.2 fusion.120
  237.5 9.2 fusion.120
  259.2 9.2 fusion.120
  280.8 9.2 fusion.120
  291.2 10.8 convolution_convert_fusion.4
  303.0 84.9 %reduce-scatter.11.cloned.1.call-done = bf16[512,2048]{1,0:T(8,128)(2,1)} async-done(((bf16[2048,2048]{1,0:T(8,128)(2,1)}), bf16[512,2048]{1,0:T(8,128)(2,1)}) %reduce-scatter.11.cloned.1.call-update) | async-done | bytes 2097168 | tf_op jit(solution)/shard_map/reduce_scatter | solution.py:124
  395.6 76.0 %all-gather.23.cloned.1.call-done = bf16[2048,2048]{1,0:T(8,128)(2,1)} async-done(((bf16[256,2048]{1,0:T(8,128)(2,1)}), bf16[2048,2048]{1,0:T(8,128)(2,1)}) %all-gather.23.cloned.1.call-update) | async-done | bytes 8388624 | tf_op jit(solution)/shard_map/all_gather | solution.py:135
  471.6 88.4 %all-gather.21.cloned.1.call-done = bf16[2048,2048]{1,0:T(8,128)(2,1)} async-done(((bf16[512,2048]{1,0:T(8,128)(2,1)}), bf16[2048,2048]{1,0:T(8,128)(2,1)}) %all-gather.21.cloned.1.call-update) | async-done | bytes 8388624 | tf_op jit(solution)/shard_map/all_gather | solution.py:138
  560.0 24.2 %fusion.64 = f32[2048,2048]{1,0:T(8,128)} fusion(bf16[2048,2048]{1,0:T(8,128)(2,1)} %all-gather.21.cloned.1.call-done, bf16[2048,2048]{1,0:T(8,128)(2,1)} %all-gather.23.cloned.1.call-done), kind=kOutput, calls=%fused_computation.124 | convolution fusion | flops 17179869184 | bytes 33554432 | tf_op jit(solution)/shard_map/dot_general | solution.py:139
  584.2 59.5 %all-gather.25.cloned.1.call-done = bf16[2048,2048]{1,0:T(8,128)(2,1)} async-done(((bf16[256,2048]{1,0:T(8,128)(2,1)}), bf16[2048,2048]{1,0:T(8,128)(2,1)}) %all-gather.25.cloned.1.call-update) | async-done | bytes 8388624 | tf_op jit(solution)/shard_map/all_gather | solution.py:136
  643.7 26.5 %convolution_convert_fusion.3 = bf16[2048,2048]{1,0:T(8,128)(2,1)} fusion(bf16[2048,2048]{1,0:T(8,128)(2,1)} %all-gather.25.cloned.1.call-done, f32[2048,2048]{1,0:T(8,128)} %fusion.64, f32[2048]{0:T(1024)S(1)} %dynamic_slice.25), kind=kOutput, calls=%fused_computation.61 | convolution fusion | flops 17226006528 | bytes 33562624 | tf_op jit(solution)/shard_map/dot_general | solution.py:20
  670.9 84.3 %reduce-scatter.13.cloned.1.call-done = bf16[512,2048]{1,0:T(8,128)(2,1)} async-done(((bf16[2048,2048]{1,0:T(8,128)(2,1)}), bf16[512,2048]{1,0:T(8,128)(2,1)}) %reduce-scatter.13.cloned.1.call-update) | async-done | bytes 2097168 | tf_op jit(solution)/shard_map/reduce_scatter | solution.py:142
  768.3 87.2 %all-gather.27.cloned.1.call-done = bf16[2048,2048]{1,0:T(8,128)(2,1)} async-done(((bf16[512,2048]{1,0:T(8,128)(2,1)}), bf16[2048,2048]{1,0:T(8,128)(2,1)}) %all-gather.27.cloned.1.call-update) | async-done | bytes 8388624 | tf_op jit(solution)/shard_map/all_gather | solution.py:155
  855.5 33.6 %convert_reduce_fusion = (f32[2048]{0:T(1024)S(1)}, bf16[2048,2048]{1,0:T(8,128)(2,1)S(1)}) fusion(f32[2048,2048]{1,0:T(8,128)} %fusion.64, f32[2048]{0:T(1024)S(1)} %dynamic_slice.25, bf16[2048,2048]{1,0:T(8,128)(2,1)} %all-gather.27.cloned.1.call-done, bf16[2048,2048]{1,0:T(8,128)(2,1)} %all-gather.25.cloned.1.call-done), kind=kOutput, calls=%fused_computation.55 | convolution fusion | flops 17276336128 | bytes 41959424 | tf_op jit(solution)/shard_map/dot_general | solution.py:156
  892.3 22.2 %convolution_convert_fusion.2 = bf16[2048,2048]{1,0:T(8,128)(2,1)} fusion(bf16[2048,2048]{1,0:T(8,128)(2,1)S(1)} %get-tuple-element.324, bf16[2048,2048]{1,0:T(8,128)(2,1)} %all-gather.23.cloned.1.call-done), kind=kOutput, calls=%fused_computation.60 | convolution fusion | flops 17184063488 | bytes 25165824 | tf_op jit(solution)/shard_map/dot_general | solution.py:20
  914.8 86.2 %reduce-scatter.15.cloned.1.call-done = bf16[512,2048]{1,0:T(8,128)(2,1)} async-done(((bf16[2048,2048]{1,0:T(8,128)(2,1)}), bf16[512,2048]{1,0:T(8,128)(2,1)}) %reduce-scatter.15.cloned.1.call-update) | async-done | bytes 2097168 | tf_op jit(solution)/shard_map/reduce_scatter | solution.py:163
  1014.8 25.1 %convolution_convert_fusion = bf16[2048,2048]{1,0:T(8,128)(2,1)} fusion(bf16[2048,2048]{1,0:T(8,128)(2,1)} %all-gather.27.cloned.1.call-done, f32[2048,2048]{1,0:T(8,128)} %fusion.64, f32[2048]{0:T(1024)S(1)} %dynamic_slice.25), kind=kOutput, calls=%fused_computation.58 | convolution fusion | flops 17226006528 | bytes 33562624 | tf_op jit(solution)/shard_map/dot_general | solution.py:14
  1042.1 23.8 %convolution_convert_fusion.1 = bf16[2048,2048]{1,0:T(8,128)(2,1)} fusion(bf16[2048,2048]{1,0:T(8,128)(2,1)} %all-gather.21.cloned.1.call-done, bf16[2048,2048]{1,0:T(8,128)(2,1)} %copy-done.27), kind=kOutput, calls=%fused_computation.59 | convolution fusion | flops 17184063488 | bytes 25165824 | tf_op jit(solution)/shard_map/dot_general | solution.py:14
  1065.9 36.4 %all-gather.29.cloned.1.call-done = bf16[2048,2048]{1,0:T(8,128)(2,1)} async-done(((bf16[512,2048]{1,0:T(8,128)(2,1)}), bf16[2048,2048]{1,0:T(8,128)(2,1)}) %all-gather.29.cloned.1.call-update) | async-done | bytes 8388624 | tf_op jit(solution)/shard_map/all_gather | solution.py:173
  1102.4 9.1 convolution_convert_fusion.9
  1115.6 208.4 %while.29 = (s32[]{:T(128)}, f32[2048,4,128]{0,2,1:T(8,128)}, f32[2048,4,128]{0,2,1:T(8,128)}, bf16[4,512,4,128]{3,1,2,0:T(8,128)(2,1)}, bf16[4,512,4,128]{3,1,2...) while((s32[]{:T(128)}, f32[2048,4,128]{0,2,1:T(8,128)}, ...), condition=%wide.region_17.18_spmd.clone, body=%wide.region_15.17_spmd.clone.sunk | while | flops 5437390848 | bytes 253296880 | solution.py:207
  1133.4 12.2 multiply_reduce_fusion.9
  1145.6 12.4 multiply_convert_fusion.6
  1185.7 12.2 multiply_reduce_fusion.9
  1197.9 12.9 multiply_convert_fusion.6
  1238.6 12.3 multiply_reduce_fusion.9
  1250.8 12.3 multiply_convert_fusion.6
  1290.9 12.1 multiply_reduce_fusion.9
  1303.0 12.0 multiply_convert_fusion.6
  1329.3 9.9 convolution_convert_fusion.5
  1343.8 9.2 fusion.46
  1356.9 9.2 fusion.47
  1366.2 9.3 fusion.48
  1375.6 12.7 fusion.65
  1396.6 17.1 %add_convert_fusion = bf16[2048,2048]{1,0:T(8,128)(2,1)} fusion(f32[2048,2048]{1,0:T(8,128)} %fusion.50, f32[2048,2048]{1,0:T(8,128)} %fusion.65, bf16[2048,512]{0,1:T(8,128)(2,1)S(1)} %bitcast.138, bf16[2048,512]{1,0:T(8,128)(2,1)} %all-gather.17.cloned.1.call-done), kind=kOutput, calls=%fused_computation.56 | convolution fusion | flops 4307550208 | bytes 46137344 | tf_op jit(solution)/shard_map/dot_general | solution.py:20
  1419.4 37.2 %all-reduce.12.cloned.1.call-done = (f32[2048]{0:T(1024)}, f32[2048]{0:T(1024)}, f32[2048]{0:T(1024)}, f32[2048]{0:T(1024)}, f32[2048]{0:T(1024)}, /*index=5*/f3...) async-done(((f32[2048]{0:T(1024)}, f32[2048]{0:T(1024)}, f32[2048]{0:T(1024)}, f32[2048]{0:T(1024)}, f32[2048]{0:T(1024)}, /*index=5*/f32[8192]{0:T(1024)}, ...) | async-done | bytes 98320
  1468.0 27.9 %reduce-scatter.25.cloned.1.call-done = bf16[256,512]{1,0:T(8,128)(2,1)} async-done(((bf16[2048,512]{1,0:T(8,128)(2,1)}), bf16[256,512]{1,0:T(8,128)(2,1)}) %reduce-scatter.25.cloned.1.call-update) | async-done | bytes 262160 | tf_op jit(solution)/shard_map/reduce_scatter | solution.py:239
  1497.7 35.6 %reduce-scatter.19.cloned.1.call-done = bf16[256,512]{0,1:T(8,128)(2,1)} async-done(((bf16[2048,512]{0,1:T(8,128)(2,1)}), bf16[256,512]{0,1:T(8,128)(2,1)}) %reduce-scatter.19.cloned.1.call-update) | async-done | bytes 262160 | tf_op jit(solution)/shard_map/reduce_scatter | solution.py:230
  1535.2 35.1 %reduce-scatter.21.cloned.1.call-done = bf16[256,512]{0,1:T(8,128)(2,1)} async-done(((bf16[2048,512]{0,1:T(8,128)(2,1)}), bf16[256,512]{0,1:T(8,128)(2,1)}) %reduce-scatter.21.cloned.1.call-update) | async-done | bytes 262160 | tf_op jit(solution)/shard_map/reduce_scatter | solution.py:233
  1572.2 34.9 %reduce-scatter.23.cloned.1.call-done = bf16[256,512]{0,1:T(8,128)(2,1)} async-done(((bf16[2048,512]{0,1:T(8,128)(2,1)}), bf16[256,512]{0,1:T(8,128)(2,1)}) %reduce-scatter.23.cloned.1.call-update) | async-done | bytes 262160 | tf_op jit(solution)/shard_map/reduce_scatter | solution.py:236
  1609.0 86.2 %reduce-scatter.17.cloned.1.call-done = bf16[512,2048]{1,0:T(8,128)(2,1)} async-done(((bf16[2048,2048]{1,0:T(8,128)(2,1)}), bf16[512,2048]{1,0:T(8,128)(2,1)}) %reduce-scatter.17.cloned.1.call-update) | async-done | bytes 2097168 | tf_op jit(solution)/shard_map/reduce_scatter | solution.py:222
  (238 shorter events, 279.4 us)
Async XLA Ops:
  7.2 34.3 %all-gather.17.cloned.1.call-start = ((), (), s32[]{:S(2)}) async-start(), calls=%async_computation.13 | async-start | bytes 2359296 | tf_op jit(solution)/shard_map/all_gather | solution.py:89
  7.9 122.3 %all-gather.11.cloned.1.call-start = ((), (), s32[]{:S(2)}) async-start(), calls=%async_computation.10 | async-start | bytes 10485760 | tf_op jit(solution)/shard_map/all_gather | solution.py:92
  8.7 152.4 %all-gather.13.cloned.1.call-start = ((), (), s32[]{:S(2)}) async-start(), calls=%async_computation.11 | async-start | bytes 2359296 | tf_op jit(solution)/shard_map/all_gather | solution.py:87
  9.4 181.7 %all-gather.15.cloned.1.call-start = ((), (), s32[]{:S(2)}) async-start(), calls=%async_computation.12 | async-start | bytes 2359296 | tf_op jit(solution)/shard_map/all_gather | solution.py:88
  10.0 281.2 %all-gather.19.cloned.1.call-start = ((), (), s32[]{:S(2)}) async-start(), calls=%async_computation.14 | async-start | bytes 2359296 | tf_op jit(solution)/shard_map/all_gather | solution.py:90
  10.6 377.3 %reduce-scatter.11.cloned.1.call-start = ((), (), s32[]{:S(2)}) async-start(), calls=%async_computation.15 | async-start | bytes 10485760 | tf_op jit(solution)/shard_map/reduce_scatter | solution.py:124
  208.8 6.4 copy-start.1
  208.8 7.0 copy-start.4
  230.6 6.3 copy-start.1
  230.6 6.9 copy-start.4
  252.3 6.3 copy-start.1
  252.3 6.9 copy-start.4
  273.9 6.3 copy-start.1
  273.9 6.9 copy-start.4
  291.2 10.8 copy-start.2
  302.0 85.9 %copy-start.7 = (bf16[512,2048]{1,0:T(8,128)(2,1)S(1)}, bf16[512,2048]{1,0:T(8,128)(2,1)}, u32[]{:S(2)}) copy-start(bf16[512,2048]{1,0:T(8,128)(2,1)} %param.22) | copy-start | bytes 6291460
  302.0 85.9 %copy-start.17 = (f32[2048]{0:T(1024)S(1)}, f32[2048]{0:T(1024)}, u32[]{:S(2)}) copy-start(f32[2048]{0:T(1024)} %param.33) | copy-start | bytes 24580
  302.0 169.6 %all-gather.23.cloned.1.call-start = ((), (), s32[]{:S(2)}) async-start(), calls=%async_computation.17 | async-start | bytes 9437184 | tf_op jit(solution)/shard_map/all_gather | solution.py:135
  302.8 88.7 %copy-start.18 = (f32[2048]{0:T(1024)S(1)}, f32[2048]{0:T(1024)}, u32[]{:S(2)}) copy-start(f32[2048]{0:T(1024)} %param.34) | copy-start | bytes 24580
  302.8 88.7 %copy-start.22 = (f32[2048]{0:T(1024)S(1)}, f32[2048]{0:T(1024)}, u32[]{:S(2)}) copy-start(f32[2048]{0:T(1024)} %param.35) | copy-start | bytes 24580
  302.8 257.2 %all-gather.21.cloned.1.call-start = ((), (), s32[]{:S(2)}) async-start(), calls=%async_computation.16 | async-start | bytes 10485760 | tf_op jit(solution)/shard_map/all_gather | solution.py:138
  394.1 249.6 %all-gather.25.cloned.1.call-start = ((), (), s32[]{:S(2)}) async-start(), calls=%async_computation.18 | async-start | bytes 9437184 | tf_op jit(solution)/shard_map/all_gather | solution.py:136
  394.8 360.4 %reduce-scatter.13.cloned.1.call-start = ((), (), s32[]{:S(2)}) async-start(), calls=%async_computation.19 | async-start | bytes 10485760 | tf_op jit(solution)/shard_map/reduce_scatter | solution.py:142
  670.2 85.0 %copy-start.24 = (f32[2048]{0:T(1024)S(1)}, f32[2048]{0:T(1024)}, u32[]{:S(2)}) copy-start(f32[2048]{0:T(1024)} %param.37) | copy-start | bytes 24580
  670.2 185.2 %all-gather.27.cloned.1.call-start = ((), (), s32[]{:S(2)}) async-start(), calls=%async_computation.20 | async-start | bytes 10485760 | tf_op jit(solution)/shard_map/all_gather | solution.py:155
  759.5 3.9 copy-start.23
  767.8 233.2 %reduce-scatter.15.cloned.1.call-start = ((), (), s32[]{:S(2)}) async-start(), calls=%async_computation.21 | async-start | bytes 10485760 | tf_op jit(solution)/shard_map/reduce_scatter | solution.py:163
  889.1 3.2 copy-start.27
  914.5 187.8 %all-gather.29.cloned.1.call-start = ((), (), s32[]{:S(2)}) async-start(), calls=%async_computation.22 | async-start | bytes 10485760 | tf_op jit(solution)/shard_map/all_gather | solution.py:173
  1001.0 7.0 copy-start.9
  1001.0 7.0 copy-start.11
  1001.0 7.0 copy-start.12
  1014.7 399.0 %reduce-scatter.29.cloned.1.call-start = ((), (), s32[]{:S(2)}) async-start(), calls=%async_computation.29 | async-start | bytes 9437184 | tf_op jit(solution)/shard_map/reduce_scatter | solution.py:245
  1039.9 376.7 %reduce-scatter.27.cloned.1.call-start = ((), (), s32[]{:S(2)}) async-start(), calls=%async_computation.28 | async-start | bytes 9437184 | tf_op jit(solution)/shard_map/reduce_scatter | solution.py:242
  1065.8 36.5 %copy-start.26 = (bf16[2048,512]{1,0:T(8,128)(2,1)S(1)}, bf16[2048,512]{1,0:T(8,128)(2,1)}, u32[]{:S(2)}) copy-start(bf16[2048,512]{1,0:T(8,128)(2,1)} %all-gather.19.cloned.1.call-done) | copy-start | bytes 6291460
  1065.9 390.7 %all-reduce.12.cloned.1.call-start = ((), (), s32[]{:S(2)}) async-start(), calls=%async_computation.30 | async-start | bytes 196608
  1111.5 4.1 copy-start.3
  1122.0 5.7 copy-start
  1172.8 5.7 copy-start
  1225.6 5.7 copy-start
  1277.9 5.7 copy-start
  1329.2 166.7 %reduce-scatter.25.cloned.1.call-start = ((), (), s32[]{:S(2)}) async-start(), calls=%async_computation.27 | async-start | bytes 2359296 | tf_op jit(solution)/shard_map/reduce_scatter | solution.py:239
  1339.2 194.2 %reduce-scatter.19.cloned.1.call-start = ((), (), s32[]{:S(2)}) async-start(), calls=%async_computation.24 | async-start | bytes 2359296 | tf_op jit(solution)/shard_map/reduce_scatter | solution.py:230
  1353.0 217.3 %reduce-scatter.21.cloned.1.call-start = ((), (), s32[]{:S(2)}) async-start(), calls=%async_computation.25 | async-start | bytes 2359296 | tf_op jit(solution)/shard_map/reduce_scatter | solution.py:233
  1366.1 241.0 %reduce-scatter.23.cloned.1.call-start = ((), (), s32[]{:S(2)}) async-start(), calls=%async_computation.26 | async-start | bytes 2359296 | tf_op jit(solution)/shard_map/reduce_scatter | solution.py:236
  1375.5 319.7 %reduce-scatter.17.cloned.1.call-start = ((), (), s32[]{:S(2)}) async-start(), calls=%async_computation.23 | async-start | bytes 10485760 | tf_op jit(solution)/shard_map/reduce_scatter | solution.py:222
  1375.6 12.7 copy-start.16
  1375.6 12.7 copy-start.25
  (16 other events, 34.1 us)
Sparse Core Ops, SparseCore 0:
  9.6 31.8 all-gather.16
  43.3 86.8 all-gather.10
  131.9 29.1 all-gather.12
  162.5 28.5 all-gather.14
  192.5 28.5 all-gather.18
  302.1 85.7 reduce-scatter.10
  389.5 82.0 all-gather.22
  474.0 85.9 all-gather.20
  561.6 82.0 all-gather.24
  670.3 84.7 reduce-scatter.12
  768.0 87.4 all-gather.26
  914.7 86.3 reduce-scatter.14
  1014.8 87.4 all-gather.28
  1104.5 89.5 reduce-scatter.28
  1196.2 87.9 reduce-scatter.26
  1329.4 127.2 all-reduce.11
  1458.7 37.1 reduce-scatter.24
  1498.6 34.6 reduce-scatter.18
  1535.6 34.6 reduce-scatter.20
  1572.5 34.5 reduce-scatter.22
  1610.2 84.9 reduce-scatter.16
where the time goes:
time: 1710 us
  waiting for transfers between devices  1020 us (60%)
  matrix products  448 us (26%)
  other arithmetic  121 us (7%)
  local copies, waits for them, and re-layouts  102 us (6%)
    dot_general x6, matrix products, contract_cols(): lax.dot_general(left, right, (((1,), (1,)), ((), ())), preferred_element_...  97.6 us
    all_gather x1, waiting for transfers between devices, per_device(): piece = lax.all_gather(tokens, 'tensor', axis=0, tiled=True)  88.7 us
    all_gather x1, waiting for transfers between devices, per_device(): piece = lax.all_gather(mid_low, 'tensor', axis=0, tiled=True)  88.4 us
    all_gather x1, waiting for transfers between devices, per_device(): lax.all_gather(grad_sum2.astype(jnp.bfloat16), 'tensor', axis=0, tiled=True)  87.2 us
    dot_general x6, matrix products, contract_rows(): lax.dot_general(left, right, (((0,), (0,)), ((), ())), preferred_element_...  86.5 us
    reduce_scatter x1, waiting for transfers between devices, per_device(): lax.psum_scatter(contract_cols(grad_pre, up_full).astype(jnp.bfloat16), '...  86.2 us
    reduce_scatter x1, waiting for transfers between devices, per_device(): lax.psum_scatter((total + contract_cols(grad_values, value_full)).astype(...  86.2 us
    reduce_scatter x1, waiting for transfers between devices, per_device(): lax.psum_scatter(contract_cols(context, out_full).astype(jnp.bfloat16), '...  84.9 us
  transfers between devices with their start and end apart: 21, of which 18 were waited for; matrix products, arithmetic and copies ran while one was open for 29% of the time, Pallas kernels for 0%

commit v1 on v0

--- a/solution.py
+++ b/solution.py
@@ -8,6 +8,28 @@
 FF = 8192
 norm_eps = 1e-06
 masked_score = -1e30
+
+
+def obtain_plate_on(obj, ndim_at):
+    block_now = list(obj.shape[1:])
+    block_now[ndim_at] *= obj.shape[0]
+    return jnp.moveaxis(obj, 0, ndim_at).reshape(block_now)
+
+
+def _touch_goods(u, mesh_ax, dim_no=0):
+    num_devices = lax.axis_size(mesh_ax)
+    in_order = list(map(lambda j: (j, (j + 1) % num_devices), range(num_devices)))
+    entries = [(idx, k0) for k0, idx in in_order]
+    all_values, arr_next = ([], [])
+    for jj in range(num_devices - 1):
+        if jj % 2 == 0:
+            all_values.append(lax.ppermute(all_values[-1] if all_values else u, mesh_ax, in_order))
+        else:
+            arr_next.append(lax.ppermute(arr_next[-1] if arr_next else u, mesh_ax, entries))
+    answer = jnp.stack([*all_values[::-1], u, *arr_next])
+    formed = lax.axis_index(mesh_ax) - len(all_values)
+    answer = answer[(jnp.arange(num_devices) - formed) % num_devices]
+    return obtain_plate_on(answer, dim_no)
 
 
 def contract_rows(left, right):
@@ -135,7 +157,7 @@
         lax.all_gather(up_weight, "dp", axis=0, tiled=True),
         lax.all_gather(down_weight, "dp", axis=0, tiled=True),
     )
-    piece = lax.all_gather(mid_low, "tensor", axis=0, tiled=True)
+    piece = _touch_goods(mid_low, "tensor")
     pre = jnp.dot(piece, up_full, preferred_element_type=jnp.float32) + bias_up
     mid_seq = piece
     activ = smooth_gate(pre).astype(jnp.bfloat16)

time: 1710 us -> 1650 us (0.965)
  waiting for transfers between devices: 1020 us -> 929 us
    ppermute x0 -> x3, waiting for transfers between devices: none -> 134 us  [the longest x2 90.4 us: _touch_goods(): lax.ppermute(all_values[-1] if all_values else u, mesh_ax, in_order)]
    all_gather x1 -> x0, waiting for transfers between devices: 88.4 us -> none  [per_device(): piece = lax.all_gather(mid_low, 'tensor', axis=0, tiled=True)]
    all_gather x1, waiting for transfers between devices: 76 us -> 0.01 us  [per_device(): lax.all_gather(up_weight, 'dp', axis=0, tiled=True)]
    all_gather x1, waiting for transfers between devices: 59.5 us -> 0.01 us  [per_device(): lax.all_gather(down_weight, 'dp', axis=0, tiled=True)]
    unnamed x22 -> x21, waiting for transfers between devices: 42 us -> 41.9 us
  transfers between devices with their start and end apart: 21 -> 23, of which waited for: 18 -> 18; matrix products, arithmetic and copies ran while one was open for 29% -> 32% of each run, Pallas kernels for 0% -> 0%
where the time goes in v1:
time: 1650 us
  waiting for transfers between devices  929 us (56%)
  matrix products  448 us (27%)
  other arithmetic  133 us (8%)
  local copies, waits for them, and re-layouts  116 us (7%)
    dot_general x6, matrix products, contract_cols(): lax.dot_general(left, right, (((1,), (1,)), ((), ())), preferred_element_...  97.6 us
    ppermute x2, waiting for transfers between devices, _touch_goods(): lax.ppermute(all_values[-1] if all_values else u, mesh_ax, in_order)  90.4 us
    all_gather x1, waiting for transfers between devices, per_device(): piece = lax.all_gather(tokens, 'tensor', axis=0, tiled=True)  88.7 us
    all_gather x1, waiting for transfers between devices, per_device(): lax.all_gather(grad_sum2.astype(jnp.bfloat16), 'tensor', axis=0, tiled=True)  87.6 us
    dot_general x6, matrix products, contract_rows(): lax.dot_general(left, right, (((0,), (0,)), ((), ())), preferred_element_...  86.6 us
    reduce_scatter x1, waiting for transfers between devices, per_device(): lax.psum_scatter(contract_cols(grad_pre, up_full).astype(jnp.bfloat16), '...  86 us
    reduce_scatter x1, waiting for transfers between devices, per_device(): lax.psum_scatter((total + contract_cols(grad_values, value_full)).astype(...  85.9 us
    reduce_scatter x1, waiting for transfers between devices, per_device(): lax.psum_scatter(contract_cols(activ, down_full).astype(jnp.bfloat16), 't...  85.6 us
  transfers between devices with their start and end apart: 23, of which 18 were waited for; matrix products, arithmetic and copies ran while one was open for 32% of the time, Pallas kernels for 0%

profile of v1, /device:TPU:0, one launch (start us, length us, event | category | flops | bytes accessed | tf_op | source)
XLA Modules:
  0.0 1648.4 jit_solution(9310466015903434492)
XLA Ops:
  12.2 29.3 %all-gather.16.cloned.1.call-done = bf16[2048,512]{1,0:T(8,128)(2,1)} async-done(((bf16[256,512]{1,0:T(8,128)(2,1)}), bf16[2048,512]{1,0:T(8,128)(2,1)}) %all-gather.16.cloned.1.call-update) | async-done | bytes 2097168 | tf_op jit(solution)/shard_map/all_gather | solution.py:111
  41.5 88.7 %all-gather.10.cloned.1.call-done = bf16[2048,2048]{1,0:T(8,128)(2,1)} async-done(((bf16[512,2048]{1,0:T(8,128)(2,1)}), bf16[2048,2048]{1,0:T(8,128)(2,1)}) %all-gather.10.cloned.1.call-update) | async-done | bytes 8388624 | tf_op jit(solution)/shard_map/all_gather | solution.py:114
  141.5 19.5 %all-gather.12.cloned.1.call-done = bf16[2048,512]{1,0:T(8,128)(2,1)} async-done(((bf16[256,512]{1,0:T(8,128)(2,1)}), bf16[2048,512]{1,0:T(8,128)(2,1)}) %all-gather.12.cloned.1.call-update) | async-done | bytes 2097168 | tf_op jit(solution)/shard_map/all_gather | solution.py:109
  161.0 9.8 add_convert_fusion.3
  175.1 16.0 all-gather.14.cloned.1.call-done
  191.1 9.9 convolution_convert_fusion.10
  204.0 87.0 %while.28 = (s32[]{:T(128)}, bf16[4,512,4,128]{3,2,1,0:T(4,128)(2,1)}, f32[4,4,512,1]{2,1,3,0:T(4,128)}, bf16[4,512,4,128]{3,1,2,0:T(8,128)(2,1)}, bf16[2048,4,1...) while((s32[]{:T(128)}, bf16[4,512,4,128]{3,2,1,0:T(4,128)(2,1)}, ...), condition=%wide.region_3.4_spmd.clone, body=%wide.region_0.3_spmd.clone.sunk | while | flops 2193883136 | bytes 132194472 | solution.py:144
  215.6 9.2 fusion.123
  237.3 9.2 fusion.123
  259.0 9.2 fusion.123
  280.6 9.2 fusion.123
  291.0 10.8 convolution_convert_fusion.4
  303.9 83.8 %reduce-scatter.11.cloned.1.call-done = bf16[512,2048]{1,0:T(8,128)(2,1)} async-done(((bf16[2048,2048]{1,0:T(8,128)(2,1)}), bf16[512,2048]{1,0:T(8,128)(2,1)}) %reduce-scatter.11.cloned.1.call-update) | async-done | bytes 2097168 | tf_op jit(solution)/shard_map/reduce_scatter | solution.py:146
  396.8 46.8 %collective-permute-done = bf16[512,2048]{1,0:T(8,128)(2,1)} collective-permute-done((bf16[512,2048]{1,0:T(8,128)(2,1)}, bf16[512,2048]{1,0:T(8,128)(2,1)}, u32[]{:S(2)}, u32[]{:S(2)}) %collective-permute-start) | collective-permute-done | bytes 2097184 | tf_op jit(solution)/shard_map/ppermute | solution.py:26
  444.9 43.6 %collective-permute-done.2 = bf16[512,2048]{1,0:T(8,128)(2,1)} collective-permute-done((bf16[512,2048]{1,0:T(8,128)(2,1)}, bf16[512,2048]{1,0:T(8,128)(2,1)}, u32[]{:S(2)}, u32[]{:S(2)}) %collective-permute-start.2) | collective-permute-done | bytes 2097184 | tf_op jit(solution)/shard_map/ppermute | solution.py:28
  488.5 43.7 %collective-permute-done.1 = bf16[512,2048]{1,0:T(8,128)(2,1)} collective-permute-done((bf16[512,2048]{1,0:T(8,128)(2,1)}, bf16[512,2048]{1,0:T(8,128)(2,1)}, u32[]{:S(2)}, u32[]{:S(2)}) %collective-permute-start.1) | collective-permute-done | bytes 2097184 | tf_op jit(solution)/shard_map/ppermute | solution.py:26
  558.4 24.2 %fusion.67 = f32[2048,2048]{1,0:T(8,128)} fusion(bf16[2048,2048]{1,0:T(8,128)(2,1)} %bitcast.146, bf16[2048,2048]{1,0:T(8,128)(2,1)} %all-gather.20.cloned.1.call-done), kind=kOutput, calls=%fused_computation.136 | convolution fusion | flops 17179869184 | bytes 33554432 | tf_op jit(solution)/shard_map/dot_general | solution.py:161
  582.6 26.5 %convolution_convert_fusion.3 = bf16[2048,2048]{1,0:T(8,128)(2,1)} fusion(bf16[2048,2048]{1,0:T(8,128)(2,1)} %all-gather.22.cloned.1.call-done, f32[2048,2048]{1,0:T(8,128)} %fusion.67, f32[2048]{0:T(1024)S(1)} %dynamic_slice.25), kind=kOutput, calls=%fused_computation.65 | convolution fusion | flops 17226006528 | bytes 33562624 | tf_op jit(solution)/shard_map/dot_general | solution.py:42
  610.1 85.6 %reduce-scatter.13.cloned.1.call-done = bf16[512,2048]{1,0:T(8,128)(2,1)} async-done(((bf16[2048,2048]{1,0:T(8,128)(2,1)}), bf16[512,2048]{1,0:T(8,128)(2,1)}) %reduce-scatter.13.cloned.1.call-update) | async-done | bytes 2097168 | tf_op jit(solution)/shard_map/reduce_scatter | solution.py:164
  708.4 87.6 %all-gather.24.cloned.1.call-done = bf16[2048,2048]{1,0:T(8,128)(2,1)} async-done(((bf16[512,2048]{1,0:T(8,128)(2,1)}), bf16[2048,2048]{1,0:T(8,128)(2,1)}) %all-gather.24.cloned.1.call-update) | async-done | bytes 8388624 | tf_op jit(solution)/shard_map/all_gather | solution.py:177
  796.0 33.6 %convert_reduce_fusion = (f32[2048]{0:T(1024)S(1)}, bf16[2048,2048]{1,0:T(8,128)(2,1)S(1)}) fusion(f32[2048,2048]{1,0:T(8,128)} %fusion.67, f32[2048]{0:T(1024)S(1)} %dynamic_slice.25, bf16[2048,2048]{1,0:T(8,128)(2,1)} %all-gather.24.cloned.1.call-done, bf16[2048,2048]{1,0:T(8,128)(2,1)} %all-gather.22.cloned.1.call-done), kind=kOutput, calls=%fused_computation.57 | convolution fusion | flops 17276336128 | bytes 41959424 | tf_op jit(solution)/shard_map/dot_general | solution.py:178
  833.0 22.2 %convolution_convert_fusion.2 = bf16[2048,2048]{1,0:T(8,128)(2,1)} fusion(bf16[2048,2048]{1,0:T(8,128)(2,1)S(1)} %get-tuple-element.324, bf16[2048,2048]{1,0:T(8,128)(2,1)} %all-gather.20.cloned.1.call-done), kind=kOutput, calls=%fused_computation.64 | convolution fusion | flops 17184063488 | bytes 25165824 | tf_op jit(solution)/shard_map/dot_general | solution.py:42
  855.6 86.0 %reduce-scatter.15.cloned.1.call-done = bf16[512,2048]{1,0:T(8,128)(2,1)} async-done(((bf16[2048,2048]{1,0:T(8,128)(2,1)}), bf16[512,2048]{1,0:T(8,128)(2,1)}) %reduce-scatter.15.cloned.1.call-update) | async-done | bytes 2097168 | tf_op jit(solution)/shard_map/reduce_scatter | solution.py:185
  955.4 25.1 %convolution_convert_fusion = bf16[2048,2048]{1,0:T(8,128)(2,1)} fusion(bf16[2048,2048]{1,0:T(8,128)(2,1)} %all-gather.24.cloned.1.call-done, f32[2048,2048]{1,0:T(8,128)} %fusion.67, f32[2048]{0:T(1024)S(1)} %dynamic_slice.25), kind=kOutput, calls=%fused_computation.62 | convolution fusion | flops 17226006528 | bytes 33562624 | tf_op jit(solution)/shard_map/dot_general | solution.py:36
  982.7 23.8 %convolution_convert_fusion.1 = bf16[2048,2048]{1,0:T(8,128)(2,1)} fusion(bf16[2048,2048]{1,0:T(8,128)(2,1)} %bitcast.147, bf16[2048,2048]{1,0:T(8,128)(2,1)} %copy-done.27), kind=kOutput, calls=%fused_computation.63 | convolution fusion | flops 17184063488 | bytes 25165824 | tf_op jit(solution)/shard_map/dot_general | solution.py:36
  1006.5 36.4 %all-gather.26.cloned.1.call-done = bf16[2048,2048]{1,0:T(8,128)(2,1)} async-done(((bf16[512,2048]{1,0:T(8,128)(2,1)}), bf16[2048,2048]{1,0:T(8,128)(2,1)}) %all-gather.26.cloned.1.call-update) | async-done | bytes 8388624 | tf_op jit(solution)/shard_map/all_gather | solution.py:195
  1043.0 9.1 convolution_convert_fusion.9
  1056.2 209.3 %while.29 = (s32[]{:T(128)}, f32[2048,4,128]{0,2,1:T(8,128)}, f32[2048,4,128]{0,2,1:T(8,128)}, bf16[4,512,4,128]{3,1,2,0:T(8,128)(2,1)}, bf16[4,512,4,128]{3,1,2...) while((s32[]{:T(128)}, f32[2048,4,128]{0,2,1:T(8,128)}, ...), condition=%wide.region_17.18_spmd.clone, body=%wide.region_15.17_spmd.clone.sunk | while | flops 5437390848 | bytes 253296880 | solution.py:229
  1073.9 12.4 multiply_reduce_fusion.9
  1086.3 12.4 multiply_convert_fusion.6
  1126.5 12.3 multiply_reduce_fusion.9
  1138.8 12.9 multiply_convert_fusion.6
  1179.6 12.4 multiply_reduce_fusion.9
  1192.0 12.3 multiply_convert_fusion.6
  1232.3 12.2 multiply_reduce_fusion.9
  1244.5 12.0 multiply_convert_fusion.6
  1270.8 9.9 convolution_convert_fusion.5
  1285.3 9.2 fusion.46
  1298.4 9.1 fusion.47
  1307.7 9.5 fusion.48
  1317.2 12.7 fusion.68
  1338.3 17.1 %add_convert_fusion = bf16[2048,2048]{1,0:T(8,128)(2,1)} fusion(f32[2048,2048]{1,0:T(8,128)} %fusion.50, f32[2048,2048]{1,0:T(8,128)} %fusion.68, bf16[2048,512]{0,1:T(8,128)(2,1)S(1)} %bitcast.145, bf16[2048,512]{1,0:T(8,128)(2,1)} %all-gather.16.cloned.1.call-done), kind=kOutput, calls=%fused_computation.58 | convolution fusion | flops 4307550208 | bytes 46137344 | tf_op jit(solution)/shard_map/dot_general | solution.py:42
  1361.0 37.2 %all-reduce.12.cloned.1.call-done = (f32[2048]{0:T(1024)}, f32[2048]{0:T(1024)}, f32[2048]{0:T(1024)}, f32[2048]{0:T(1024)}, f32[2048]{0:T(1024)}, /*index=5*/f3...) async-done(((f32[2048]{0:T(1024)}, f32[2048]{0:T(1024)}, f32[2048]{0:T(1024)}, f32[2048]{0:T(1024)}, f32[2048]{0:T(1024)}, /*index=5*/f32[8192]{0:T(1024)}, ...) | async-done | bytes 98320
  1409.6 28.0 %reduce-scatter.25.cloned.1.call-done = bf16[256,512]{1,0:T(8,128)(2,1)} async-done(((bf16[2048,512]{1,0:T(8,128)(2,1)}), bf16[256,512]{1,0:T(8,128)(2,1)}) %reduce-scatter.25.cloned.1.call-update) | async-done | bytes 262160 | tf_op jit(solution)/shard_map/reduce_scatter | solution.py:261
  1439.3 35.6 %reduce-scatter.19.cloned.1.call-done = bf16[256,512]{0,1:T(8,128)(2,1)} async-done(((bf16[2048,512]{0,1:T(8,128)(2,1)}), bf16[256,512]{0,1:T(8,128)(2,1)}) %reduce-scatter.19.cloned.1.call-update) | async-done | bytes 262160 | tf_op jit(solution)/shard_map/reduce_scatter | solution.py:252
  1476.8 34.9 %reduce-scatter.21.cloned.1.call-done = bf16[256,512]{0,1:T(8,128)(2,1)} async-done(((bf16[2048,512]{0,1:T(8,128)(2,1)}), bf16[256,512]{0,1:T(8,128)(2,1)}) %reduce-scatter.21.cloned.1.call-update) | async-done | bytes 262160 | tf_op jit(solution)/shard_map/reduce_scatter | solution.py:255
  1513.6 35.0 %reduce-scatter.23.cloned.1.call-done = bf16[256,512]{0,1:T(8,128)(2,1)} async-done(((bf16[2048,512]{0,1:T(8,128)(2,1)}), bf16[256,512]{0,1:T(8,128)(2,1)}) %reduce-scatter.23.cloned.1.call-update) | async-done | bytes 262160 | tf_op jit(solution)/shard_map/reduce_scatter | solution.py:258
  1550.6 85.9 %reduce-scatter.17.cloned.1.call-done = bf16[512,2048]{1,0:T(8,128)(2,1)} async-done(((bf16[2048,2048]{1,0:T(8,128)(2,1)}), bf16[512,2048]{1,0:T(8,128)(2,1)}) %reduce-scatter.17.cloned.1.call-update) | async-done | bytes 2097168 | tf_op jit(solution)/shard_map/reduce_scatter | solution.py:244
  (248 shorter events, 309.9 us)
Async XLA Ops:
  7.2 34.3 %all-gather.16.cloned.1.call-start = ((), (), s32[]{:S(2)}) async-start(), calls=%async_computation.13 | async-start | bytes 2359296 | tf_op jit(solution)/shard_map/all_gather | solution.py:111
  7.9 122.3 %all-gather.10.cloned.1.call-start = ((), (), s32[]{:S(2)}) async-start(), calls=%async_computation.10 | async-start | bytes 10485760 | tf_op jit(solution)/shard_map/all_gather | solution.py:114
  8.7 152.4 %all-gather.12.cloned.1.call-start = ((), (), s32[]{:S(2)}) async-start(), calls=%async_computation.11 | async-start | bytes 2359296 | tf_op jit(solution)/shard_map/all_gather | solution.py:109
  9.4 181.7 %all-gather.14.cloned.1.call-start = ((), (), s32[]{:S(2)}) async-start(), calls=%async_computation.12 | async-start | bytes 2359296 | tf_op jit(solution)/shard_map/all_gather | solution.py:110
  10.0 281.0 %all-gather.18.cloned.1.call-start = ((), (), s32[]{:S(2)}) async-start(), calls=%async_computation.14 | async-start | bytes 2359296 | tf_op jit(solution)/shard_map/all_gather | solution.py:112
  10.6 377.2 %reduce-scatter.11.cloned.1.call-start = ((), (), s32[]{:S(2)}) async-start(), calls=%async_computation.15 | async-start | bytes 10485760 | tf_op jit(solution)/shard_map/reduce_scatter | solution.py:146
  208.6 6.4 copy-start.1
  208.6 7.0 copy-start.4
  230.4 6.3 copy-start.1
  230.4 6.9 copy-start.4
  252.1 6.3 copy-start.1
  252.1 6.9 copy-start.4
  273.7 6.3 copy-start.1
  273.7 6.9 copy-start.4
  291.0 10.8 copy-start.2
  301.8 85.9 %copy-start.7 = (bf16[512,2048]{1,0:T(8,128)(2,1)S(1)}, bf16[512,2048]{1,0:T(8,128)(2,1)}, u32[]{:S(2)}) copy-start(bf16[512,2048]{1,0:T(8,128)(2,1)} %param.22) | copy-start | bytes 6291460
  301.8 85.9 %copy-start.17 = (f32[2048]{0:T(1024)S(1)}, f32[2048]{0:T(1024)}, u32[]{:S(2)}) copy-start(f32[2048]{0:T(1024)} %param.33) | copy-start | bytes 24580
  301.9 256.5 %all-gather.20.cloned.1.call-start = ((), (), s32[]{:S(2)}) async-start(), calls=%async_computation.16 | async-start | bytes 9437184 | tf_op jit(solution)/shard_map/all_gather | solution.py:157
  302.6 280.0 %all-gather.22.cloned.1.call-start = ((), (), s32[]{:S(2)}) async-start(), calls=%async_computation.17 | async-start | bytes 9437184 | tf_op jit(solution)/shard_map/all_gather | solution.py:158
  303.4 88.0 %copy-start.18 = (f32[2048]{0:T(1024)S(1)}, f32[2048]{0:T(1024)}, u32[]{:S(2)}) copy-start(f32[2048]{0:T(1024)} %param.34) | copy-start | bytes 24580
  303.4 88.0 %copy-start.22 = (f32[2048]{0:T(1024)S(1)}, f32[2048]{0:T(1024)}, u32[]{:S(2)}) copy-start(f32[2048]{0:T(1024)} %param.35) | copy-start | bytes 24580
  303.4 392.3 %reduce-scatter.13.cloned.1.call-start = ((), (), s32[]{:S(2)}) async-start(), calls=%async_computation.18 | async-start | bytes 10485760 | tf_op jit(solution)/shard_map/reduce_scatter | solution.py:164
  393.9 49.7 %collective-permute-start = (bf16[512,2048]{1,0:T(8,128)(2,1)}, bf16[512,2048]{1,0:T(8,128)(2,1)}, u32[]{:S(2)}, u32[]{:S(2)}) collective-permute-start(bf16[512,2048]{1,0:T(8,128)(2,1)} %fusion.44), channel_id=1, source_target_pairs={{0,1},{1,2},{2,3},{3,0},{4,5},{5,6},{6,7},{7,4},{8,9},{9,10},{10,1... | collective-permute-start | bytes 6291464 | tf_op jit(solution)/shard_map/ppermute | solution.py:26
  395.4 93.2 %collective-permute-start.2 = (bf16[512,2048]{1,0:T(8,128)(2,1)}, bf16[512,2048]{1,0:T(8,128)(2,1)}, u32[]{:S(2)}, u32[]{:S(2)}) collective-permute-start(bf16[512,2048]{1,0:T(8,128)(2,1)} %fusion.44), channel_id=1, source_target_pairs={{1,0},{2,1},{3,2},{0,3},{5,4},{6,5},{7,6},{4,7},{9,8},{10,9},{11,1... | collective-permute-start | bytes 6291464 | tf_op jit(solution)/shard_map/ppermute | solution.py:28
  443.6 88.6 %collective-permute-start.1 = (bf16[512,2048]{1,0:T(8,128)(2,1)}, bf16[512,2048]{1,0:T(8,128)(2,1)}, u32[]{:S(2)}, u32[]{:S(2)}) collective-permute-start(bf16[512,2048]{1,0:T(8,128)(2,1)} %collective-permute-done), channel_id=1, source_target_pairs={{0,1},{1,2},{2,3},{3,0},{4,5},{5,6},{6,7},{7,4},{8,9},{9,10},{10,1... | collective-permute-start | bytes 6291464 | tf_op jit(solution)/shard_map/ppermute | solution.py:26
  609.2 86.6 %copy-start.24 = (f32[2048]{0:T(1024)S(1)}, f32[2048]{0:T(1024)}, u32[]{:S(2)}) copy-start(f32[2048]{0:T(1024)} %param.37) | copy-start | bytes 24580
  609.2 186.8 %all-gather.24.cloned.1.call-start = ((), (), s32[]{:S(2)}) async-start(), calls=%async_computation.19 | async-start | bytes 10485760 | tf_op jit(solution)/shard_map/all_gather | solution.py:177
  708.4 233.2 %reduce-scatter.15.cloned.1.call-start = ((), (), s32[]{:S(2)}) async-start(), calls=%async_computation.20 | async-start | bytes 10485760 | tf_op jit(solution)/shard_map/reduce_scatter | solution.py:185
  855.2 187.8 %all-gather.26.cloned.1.call-start = ((), (), s32[]{:S(2)}) async-start(), calls=%async_computation.21 | async-start | bytes 10485760 | tf_op jit(solution)/shard_map/all_gather | solution.py:195
  941.6 7.0 copy-start.9
  941.6 7.0 copy-start.11
  941.6 7.0 copy-start.12
  955.3 400.1 %reduce-scatter.29.cloned.1.call-start = ((), (), s32[]{:S(2)}) async-start(), calls=%async_computation.28 | async-start | bytes 9437184 | tf_op jit(solution)/shard_map/reduce_scatter | solution.py:267
  980.5 377.7 %reduce-scatter.27.cloned.1.call-start = ((), (), s32[]{:S(2)}) async-start(), calls=%async_computation.27 | async-start | bytes 9437184 | tf_op jit(solution)/shard_map/reduce_scatter | solution.py:264
  1006.4 36.5 %copy-start.26 = (bf16[2048,512]{1,0:T(8,128)(2,1)S(1)}, bf16[2048,512]{1,0:T(8,128)(2,1)}, u32[]{:S(2)}) copy-start(bf16[2048,512]{1,0:T(8,128)(2,1)} %all-gather.18.cloned.1.call-done) | copy-start | bytes 6291460
  1006.5 391.7 %all-reduce.12.cloned.1.call-start = ((), (), s32[]{:S(2)}) async-start(), calls=%async_computation.29 | async-start | bytes 196608
  1052.0 4.2 copy-start.3
  1062.4 5.8 copy-start
  1113.4 5.8 copy-start
  1166.5 5.8 copy-start
  1219.2 5.8 copy-start
  1270.8 166.8 %reduce-scatter.25.cloned.1.call-start = ((), (), s32[]{:S(2)}) async-start(), calls=%async_computation.26 | async-start | bytes 2359296 | tf_op jit(solution)/shard_map/reduce_scatter | solution.py:261
  1280.7 194.3 %reduce-scatter.19.cloned.1.call-start = ((), (), s32[]{:S(2)}) async-start(), calls=%async_computation.23 | async-start | bytes 2359296 | tf_op jit(solution)/shard_map/reduce_scatter | solution.py:252
  1294.5 217.2 %reduce-scatter.21.cloned.1.call-start = ((), (), s32[]{:S(2)}) async-start(), calls=%async_computation.24 | async-start | bytes 2359296 | tf_op jit(solution)/shard_map/reduce_scatter | solution.py:255
  1307.6 241.1 %reduce-scatter.23.cloned.1.call-start = ((), (), s32[]{:S(2)}) async-start(), calls=%async_computation.25 | async-start | bytes 2359296 | tf_op jit(solution)/shard_map/reduce_scatter | solution.py:258
  1317.2 319.3 %reduce-scatter.17.cloned.1.call-start = ((), (), s32[]{:S(2)}) async-start(), calls=%async_computation.22 | async-start | bytes 10485760 | tf_op jit(solution)/shard_map/reduce_scatter | solution.py:244
  1317.2 12.7 copy-start.16
  1317.2 12.7 copy-start.25
  (18 other events, 41.3 us)
Sparse Core Ops, SparseCore 0:
  9.6 31.8 all-gather.15
  43.3 86.8 all-gather.9
  131.9 29.1 all-gather.11
  162.5 28.5 all-gather.13
  192.5 28.5 all-gather.17
  302.0 85.7 reduce-scatter.10
  389.3 82.0 all-gather.19
  473.0 80.5 all-gather.21
  609.3 86.3 reduce-scatter.12
  708.5 87.4 all-gather.23
  855.3 86.2 reduce-scatter.14
  955.4 87.4 all-gather.25
  1045.2 89.5 reduce-scatter.28
  1137.0 87.9 reduce-scatter.26
  1270.9 127.2 all-reduce.11
  1400.3 37.1 reduce-scatter.24
  1440.2 34.6 reduce-scatter.18
  1477.1 34.5 reduce-scatter.20
  1514.0 34.5 reduce-scatter.22
  1551.6 84.8 reduce-scatter.16
